TPU v7x, 32 devices: a whole 2x2x4 slice. The times are simulated.
32 devices in a mesh: groups: 2 (over x), seq: 16 (over z, y, core).
Axes of the slice: x: 2, y: 2, z: 4, core: 2. Of those that a mesh axis runs over, the one named last changes fastest.
Arguments:
- enc_input: bfloat16 [8192, 1408], P(('groups', 'seq')), parts along dimension 0, may hold values from -6 to 6
- enc_weight: bfloat16 [2816, 1536], P('seq'), may hold values from -0.109375 to 0.109375
- norm_gain: float32 [1536], replicated, may hold values from 0.5 to 1.5
- q_weight: bfloat16 [1536, 1024], replicated, may hold values from -1 to 1
- kv_weight: bfloat16 [1536, 320], replicated, may hold values from -1 to 1
- out_weight: bfloat16 [1536, 1536], replicated, may hold values from -0.15625 to 0.15625
- dec_weight: float32 [3, 1536], replicated, may hold values from -3 to 3
- track_weight: bfloat16 [192, 1536], P('seq'), may hold values from -0.15625 to 0.15625
- track_grad: bfloat16 [4096, 192], P('groups', 'seq'), parts along dimension 0, may hold values from -6 to 6
- track_index: int32 [384], P('groups'), parts along dimension 0, may hold values from 0 to 191, each once
- track_mask: int32 [384], P('groups'), parts along dimension 0, may hold values 0 or 1
Outputs:
- trunk_out: bfloat16 [4096, 1536], P(('groups', 'seq')), parts along dimension 0
- skip_grad: bfloat16 [4096, 1536], P(('groups', 'seq')), parts along dimension 0
- dec_weight_grad: float32 [6, 1536], P('groups'), parts along dimension 0
There are 2 independent parts, one for each index of `groups`. A program takes and returns all parts, laid end to end along the dimension named above; an argument that names none is the same for every part. Nothing has to cross between parts.
Inputs may be any that keep to these rules, and one draw needn't show every extreme that they name: `track_index`: names every track once.
All inputs are finite; a program needn't handle non-finite values.
Results may differ from a plain program's by a relative error of at most 0.02.
Values may be sent and summed in bfloat16 or wider, within the bound.
No kernel may reach another device: no remote copies, remote signals or barrier semaphores. Data moves between devices by JAX's collectives and lax.ppermute only.
A program may use at most 128 MiB of HBM per device.

v0:
```python
import math
import jax
import jax.numpy as jnp
from jax import lax
from jax.sharding import PartitionSpec as P

HEADS = 8
QK = 128
VDIM = 192
DILATION_SPAN = 8


def with_halo(cells, sides, width):
    for axis, dim in sides:
        count = lax.axis_size(axis)
        ends = count - 1
        head = lax.slice_in_dim(cells, 0, width, axis=dim)
        tail = lax.slice_in_dim(cells, cells.shape[dim] - width, cells.shape[dim], axis=dim)
        cells = jnp.concatenate(
            [
                lax.ppermute(tail, axis, [(i, (i + 1) % count) for i in range(ends)]),
                cells,
                lax.ppermute(head, axis, [((i + 1) % count, i) for i in range(ends)]),
            ],
            axis=dim,
        )
    return cells


def gelu_tanh(values):
    return jax.nn.gelu(values, approximate=True)


def attention(tokens, tok_f, norm_gain, q_weight, kv_weight, out_weight):
    token_rows = tokens.shape[0]
    normed = (
        tok_f * lax.rsqrt(jnp.mean(tok_f * tok_f, axis=-1, keepdims=True) + 1e-06) * norm_gain
    ).astype(jnp.bfloat16)
    query = jnp.dot(normed, q_weight, preferred_element_type=jnp.float32).astype(jnp.bfloat16)
    keyval = jnp.dot(normed, kv_weight, preferred_element_type=jnp.float32).astype(jnp.bfloat16)
    query_rows = query.reshape(token_rows * HEADS, QK)

    def block_update(carry, key_block):
        running_max, running_sum, weighted = carry
        scores = lax.dot_general(
            query_rows,
            key_block[:, :QK],
            (((1,), (1,)), ((), ())),
            preferred_element_type=jnp.float32,
        ) * QK ** (-0.5)
        new_max = jnp.maximum(running_max, jnp.max(scores, axis=1))
        shrink = jnp.exp(running_max - new_max)
        expw = jnp.exp(scores - new_max[:, None])
        running_sum = running_sum * shrink + jnp.sum(expw, axis=1)
        weighted = weighted * shrink[:, None] + jnp.dot(
            expw.astype(jnp.bfloat16), key_block[:, QK:], preferred_element_type=jnp.float32
        )
        return (new_max, running_sum, weighted)

    start_state = (
        jnp.full((token_rows * HEADS,), -1e30, jnp.float32),
        jnp.zeros((token_rows * HEADS,), jnp.float32),
        jnp.zeros((token_rows * HEADS, VDIM), jnp.float32),
    )
    carry = start_state
    piece = lax.all_gather(keyval, "seq", axis=0, tiled=True)
    count = piece.shape[0]

    def step_fn(inner, key_block):
        return (block_update(inner, key_block), 0)

    carry, unused = lax.scan(step_fn, carry, piece.reshape(count // 128, 128, piece.shape[1]))
    running_max, running_sum, weighted = carry
    context = (
        (weighted / running_sum[:, None]).reshape(token_rows, HEADS * VDIM).astype(jnp.bfloat16)
    )
    return (tok_f + jnp.dot(context, out_weight, preferred_element_type=jnp.float32)).astype(
        jnp.bfloat16
    )


def decoder_back(tok_f, dec_weight, track_weight, track_grad, track_index, track_mask):
    token_rows = tok_f.shape[0]
    exchanged = lax.all_to_all(track_grad, "seq", split_axis=0, concat_axis=1, tiled=True)
    masked = exchanged * track_mask.astype(jnp.bfloat16)[None, :]
    every_row = lax.all_gather(track_weight, "seq", axis=0, tiled=True)
    selected = jnp.take(every_row, track_index, axis=0)
    head_f = jnp.dot(masked, selected, preferred_element_type=jnp.float32)
    head_gradient = head_f.astype(jnp.bfloat16)
    padded_input = with_halo(head_gradient, (("seq", 0),), DILATION_SPAN).astype(jnp.float32)
    skip_act, pullback = jax.vjp(gelu_tanh, tok_f)
    convback = jnp.zeros(tok_f.shape, jnp.float32)
    tap_terms = []
    for shift_amount in range(3):
        shifted_rows = padded_input[
            DILATION_SPAN * (2 - shift_amount) : DILATION_SPAN * (2 - shift_amount) + token_rows
        ]
        convback = convback + dec_weight[shift_amount][None, :] * shifted_rows
        tap_terms.append(jnp.sum(skip_act * shifted_rows, axis=0))
    skip_grad = pullback(convback)[0].astype(jnp.bfloat16)
    summed = lax.psum(jnp.stack(tap_terms, axis=0), "seq")
    dec_weight_grad = summed / jnp.float32(math.sqrt(token_rows * lax.axis_size("seq")))
    return (skip_grad, dec_weight_grad)


def shards(
    enc_input,
    enc_weight,
    norm_gain,
    q_weight,
    kv_weight,
    out_weight,
    dec_weight,
    track_weight,
    track_grad,
    track_index,
    track_mask,
):
    token_rows = enc_input.shape[0] // 2
    patches = enc_input.reshape(token_rows, 2 * enc_input.shape[1])
    tok_sum = jnp.dot(
        patches,
        lax.all_gather(enc_weight, "seq", axis=0, tiled=True),
        preferred_element_type=jnp.float32,
    )
    tokens = tok_sum.astype(jnp.bfloat16)
    tok_f = tokens.astype(jnp.float32)
    trunk_out = attention(tokens, tok_f, norm_gain, q_weight, kv_weight, out_weight)
    skip_grad, dec_weight_grad = decoder_back(
        tok_f, dec_weight, track_weight, track_grad, track_index, track_mask
    )
    return (trunk_out, skip_grad, dec_weight_grad)


def solution(mesh):
    return jax.shard_map(
        shards,
        mesh=mesh,
        in_specs=(
            P(("groups", "seq"), None),
            P("seq", None),
            P(),
            P(),
            P(),
            P(),
            P(),
            P("seq", None),
            P("groups", "seq"),
            P("groups"),
            P("groups"),
        ),
        out_specs=(P(("groups", "seq"), None), P(("groups", "seq"), None), P("groups", None)),
        check_vma=False,
    )
```

profile of v0, /device:TPU:0, one launch (start us, length us, event | category | flops | bytes accessed | tf_op | source)
XLA Modules:
  0.0 272.7 jit_solution(8789962556055584525)
XLA Ops:
  9.6 7.4 %all-to-all-start = ((bf16[16,128,12]{1,2,0:T(8,128)(2,1)}), bf16[16,128,12]{1,2,0:T(8,128)(2,1)S(1)}, u32[]{:S(2)}, u32[]{:S(2)}) async-start(bf16[16,128,12]{1,2,0:T(8,128)(2,1)} %copy.20), calls=%async_computation | async-start | bytes 131072 | tf_op jit(solution)/shard_map/all_to_all | solution.py:84
  17.1 30.1 %all-gather = bf16[16,12,1536]{2,1,0:T(8,128)(2,1)} all-gather(bf16[1,12,1536]{2,1,0:T(8,128)(2,1)} %bitcast.28), channel_id=1, replica_groups=mesh['groups'=2,'seq'=16] {'seq'}, dimensions={0}, use_global_device_ids=true | all-gather | bytes 626688 | tf_op jit(solution)/shard_map/all_gather | solution.py:86
  47.2 2.0 reshape.51
  51.3 3.6 %gather_fusion = bf16[192,1536]{1,0:T(8,128)(2,1)} fusion(bf16[192,1536]{1,0:T(8,128)(2,1)} %reshape.51, s32[1024]{0:T(1024)S(1)} %pad_clamp_fusion), kind=kCustom, calls=%fused_computation | custom fusion | bytes 1180416 | tf_op jit(solution)/shard_map/jit(_take)/gather | solution.py:87
  57.7 2.8 %collective-permute-start = (bf16[8,1536]{1,0:T(8,128)(2,1)}, bf16[8,1536]{1,0:T(8,128)(2,1)}, u32[]{:S(2)}, u32[]{:S(2)}) collective-permute-start(bf16[8,1536]{1,0:T(8,128)(2,1)} %get-tuple-element.101), channel_id=1, source_target_pairs={{0,1},{1,2},{2,3},{3,4},{4,5},{5,6},{6,7},{7,8},{8,9},{9,10},{10,1... | collective-permute-start | bytes 73736 | tf_op jit(solution)/shard_map/ppermute | solution.py:21
  61.7 1.5 slice_reduce_fusion.2
  63.2 2.1 reshape.38
  65.4 1.8 maximum_convert_fusion
  67.2 26.1 %all-gather.4.cloned.1.call-done = bf16[2816,1536]{1,0:T(8,128)(2,1)} async-done(((bf16[176,1536]{1,0:T(8,128)(2,1)}), bf16[2816,1536]{1,0:T(8,128)(2,1)}) %all-gather.4.cloned.1.call-update) | async-done | bytes 8650768 | tf_op jit(solution)/shard_map/all_gather | solution.py:123
  93.3 7.5 %multiply_reduce_fusion.3 = (f32[1536]{0:T(1024)S(1)}, f32[1536]{0:T(1024)S(1)}, f32[1536]{0:T(1024)S(1)}, f32[128]{0:T(128)S(1)}, bf16[128,1536]{1,0:T(8,128)(2,1)}, /*index=5*/f32[128,1536]{1,0:T(8,128)S(1)}) fusion(f32[144,1536]{1,0:T(8,128)} %maximum_convert_fusion, f32[1536]{0:T(1024)S(1)} %get-tuple-element.82, f32[1536]{0:T(1024)} %get-tuple-element.83, ...), kind=kOutput, calls=%fused_computation.34 | convolution fusion | flops 1114172800 | bytes 12947968 | tf_op jit(solution)/shard_map/dot_general | solution.py:121
  102.8 2.5 convolution_convert_fusion.2
  106.4 59.2 %psum.7 = f32[3,1536]{1,0:T(4,128)S(1)} all-reduce(f32[3,1536]{1,0:T(4,128)S(1)} %pad_maximum_fusion), channel_id=1, replica_groups=mesh['groups'=2,'seq'=16] {'seq'}, use_global_device_ids=true, to_apply=%region_8.9 | all-reduce | flops 4608 | bytes 36864 | tf_op jit(solution)/shard_map/psum | solution.py:101
  166.2 2.6 copy.21
  168.7 89.4 %while.15 = (s32[]{:T(128)}, f32[1024]{0:T(1024)S(1)}, f32[1024]{0:T(1024)S(1)}, f32[1024,192]{0,1:T(8,128)}, bf16[16,128,320]{2,1,0:T(8,128)(2,1)}, /*index=5*/bf16[1024,128]{1,0:T(8,128)(2,1)S(1)}, s32[]{:T(128)}, s32[]{:T(128)}) while((s32[]{:T(128)}, f32[1024]{0:T(1024)S(1)}, f32[1024]{0:T(1024)S(1)}, f32[1024,192]{0,1:T(8,128)}, ...), condition=%wide.region_4.5_spmd.clone, body=%wide.region_1.4_spmd.clone.sunk | while | flops 85267456 | bytes 3735653 | solution.py:72
  171.9 2.2 convolution_add_fusion.3
  177.2 2.5 convolution_add_fusion.3
  182.8 2.5 convolution_add_fusion.3
  188.4 2.5 convolution_add_fusion.3
  194.0 2.5 convolution_add_fusion.3
  199.6 2.5 convolution_add_fusion.3
  205.2 2.5 convolution_add_fusion.3
  210.8 2.5 convolution_add_fusion.3
  216.4 2.5 convolution_add_fusion.3
  222.0 2.5 convolution_add_fusion.3
  227.6 2.5 convolution_add_fusion.3
  233.2 2.5 convolution_add_fusion.3
  238.8 2.5 convolution_add_fusion.3
  244.4 2.5 convolution_add_fusion.3
  250.0 2.5 convolution_add_fusion.3
  255.6 2.5 convolution_add_fusion.3
  260.3 1.5 convert_element_type.46
  261.8 4.1 %fusion.8 = bf16[128,1536]{1,0:T(8,128)(2,1)} fusion(f32[128,1536]{1,0:T(8,128)} %copy-done.1, bf16[128,1536]{1,0:T(8,128)(2,1)S(1)} %convert_element_type.46, bf16[1536,1536]{1,0:T(8,128)(2,1)} %param.18), kind=kOutput, calls=%fused_computation.19 | convolution fusion | flops 604372992 | bytes 6291456 | tf_op jit(solution)/shard_map/dot_general | solution.py:77
  (136 shorter events, 64.0 us)
Async XLA Ops:
  7.2 95.6 %copy-start = (bf16[1536,1024]{1,0:T(8,128)(2,1)S(1)}, bf16[1536,1024]{1,0:T(8,128)(2,1)}, u32[]{:S(2)}) copy-start(bf16[1536,1024]{1,0:T(8,128)(2,1)} %param.16) | copy-start | bytes 9437188
  7.2 86.1 %all-gather.4.cloned.1.call-start = ((), (), s32[]{:S(2)}) async-start(), calls=%async_computation.1 | async-start | bytes 9191424 | tf_op jit(solution)/shard_map/all_gather | solution.py:123
  9.6 45.3 %all-to-all-start = ((bf16[16,128,12]{1,2,0:T(8,128)(2,1)}), bf16[16,128,12]{1,2,0:T(8,128)(2,1)S(1)}, u32[]{:S(2)}, u32[]{:S(2)}) async-start(bf16[16,128,12]{1,2,0:T(8,128)(2,1)} %copy.20), calls=%async_computation | async-start | bytes 131072 | tf_op jit(solution)/shard_map/all_to_all | solution.py:84
  17.0 149.2 %all-gather.6.cloned.1.call-start = ((), (), s32[]{:S(2)}) async-start(), calls=%async_computation.2 | async-start | bytes 1392640 | tf_op jit(solution)/shard_map/all_gather | solution.py:66
  57.7 7.7 %collective-permute-start = (bf16[8,1536]{1,0:T(8,128)(2,1)}, bf16[8,1536]{1,0:T(8,128)(2,1)}, u32[]{:S(2)}, u32[]{:S(2)}) collective-permute-start(bf16[8,1536]{1,0:T(8,128)(2,1)} %get-tuple-element.101), channel_id=1, source_target_pairs={{0,1},{1,2},{2,3},{3,4},{4,5},{5,6},{6,7},{7,8},{8,9},{9,10},{10,1... | collective-permute-start | bytes 73736 | tf_op jit(solution)/shard_map/ppermute | solution.py:21
  60.5 4.9 %collective-permute-start.1 = (bf16[8,1536]{1,0:T(8,128)(2,1)}, bf16[8,1536]{1,0:T(8,128)(2,1)}, u32[]{:S(2)}, u32[]{:S(2)}) collective-permute-start(bf16[8,1536]{1,0:T(8,128)(2,1)} %get-tuple-element.102), channel_id=1, source_target_pairs={{1,0},{2,1},{3,2},{4,3},{5,4},{6,5},{7,6},{8,7},{9,8},{10,9},{11,1... | collective-permute-start | bytes 73736 | tf_op jit(solution)/shard_map/ppermute | solution.py:23
  93.3 8.3 %copy-start.2 = (bf16[1536,320]{0,1:T(8,128)(2,1)S(1)}, bf16[1536,320]{0,1:T(8,128)(2,1)}, u32[]{:S(2)}) copy-start(bf16[1536,320]{0,1:T(8,128)(2,1)} %param.17) | copy-start | bytes 2949124
  93.3 8.3 %copy-start.3 = (f32[1536]{0:T(1024)S(1)}, f32[1536]{0:T(1024)}, u32[]{:S(2)}) copy-start(f32[1536]{0:T(1024)} %param.15) | copy-start | bytes 18436
  100.7 0.9 copy-start.1
Sparse Core Ops, SparseCore 0:
  10.3 82.9 all-gather.3
  102.9 36.2 all-gather.5
where the time goes:
time: 275 us; the launch traced here: 273 us
  blocking collectives  89.3 us (32%)
  matrix products  72.9 us (27%)
  local copies, waits for them, and re-layouts  33.7 us (12%)
  waiting for transfers between devices  26.8 us (10%)
  other arithmetic  24.2 us (9%)
  between operations  14.2 us (5%)
  starting transfers between devices  11.6 us (4%)
    psum x1, blocking collectives, decoder_back(): summed = lax.psum(jnp.stack(tap_terms, axis=0), 'seq')  59.2 us
    dot_general x16, matrix products, block_update(): jnp.dot(expw.astype(jnp.bfloat16), key_block[:, QK:], preferred_element_t...  39.6 us
    all_gather x1, blocking collectives, decoder_back(): every_row = lax.all_gather(track_weight, 'seq', axis=0, tiled=True)  30.1 us
    all_gather x1, waiting for transfers between devices, shards(): lax.all_gather(enc_weight, 'seq', axis=0, tiled=True)  26.1 us
    reduce_sum x16, other arithmetic, block_update(): running_sum = running_sum * shrink + jnp.sum(expw, axis=1)  18.2 us
    dot_general x16, matrix products, block_update(): lax.dot_general(query_rows, key_block[:, :QK], (((1,), (1,)), ((), ())),...  16.7 us
    squeeze x16, local copies, waits for them, and re-layouts, attention(): lax.scan(step_fn, carry, piece.reshape(count // 128, 128, piece.shape[1]))  14.4 us
    dot_general x1, matrix products, shards(): jnp.dot(patches, lax.all_gather(enc_weight, 'seq', axis=0, tiled=True), p...  7.46 us
  transfers between devices with their start and end apart: 5, of which 1 were waited for; matrix products, arithmetic and copies ran while one was open for 8% of the time, Pallas kernels for 0%

commit v1 on v0

--- a/solution.py
+++ b/solution.py
@@ -8,6 +8,18 @@
 QK = 128
 VDIM = 192
 DILATION_SPAN = 8
+
+
+def gather_by_bits(x, axis, dim):
+    ways, here = (lax.axis_size(axis), lax.axis_index(axis))
+    grown, reach = (x, 1)
+    while reach < ways:
+        theirs = lax.ppermute(grown, axis, [(d, d ^ reach) for d in range(ways)])
+        mine_first = jnp.concatenate([grown, theirs], axis=dim)
+        theirs_first = jnp.concatenate([theirs, grown], axis=dim)
+        grown = jnp.where(here & reach == 0, mine_first, theirs_first)
+        reach = 2 * reach
+    return grown
 
 
 def with_halo(cells, sides, width):
@@ -119,9 +131,7 @@
     token_rows = enc_input.shape[0] // 2
     patches = enc_input.reshape(token_rows, 2 * enc_input.shape[1])
     tok_sum = jnp.dot(
-        patches,
-        lax.all_gather(enc_weight, "seq", axis=0, tiled=True),
-        preferred_element_type=jnp.float32,
+        patches, gather_by_bits(enc_weight, "seq", 0), preferred_element_type=jnp.float32
     )
     tokens = tok_sum.astype(jnp.bfloat16)
     tok_f = tokens.astype(jnp.float32)

time: 275 us -> 505 us (1.84)
  blocking collectives: 89.3 us -> 258 us
  waiting for transfers between devices: 26.8 us -> 73.5 us
  other arithmetic: 24.2 us -> 33.6 us
    all_gather x1, blocking collectives: 30.1 us -> 194 us  [decoder_back(): every_row = lax.all_gather(track_weight, 'seq', axis=0, tiled=True)]
    ppermute x0 -> x4, waiting for transfers between devices: none -> 73.5 us  [gather_by_bits(): theirs = lax.ppermute(grown, axis, [(d, d ^ reach) for d in range(ways)])]
    all_gather x1 -> x0, waiting for transfers between devices: 26.1 us -> none  [shards(): lax.all_gather(enc_weight, 'seq', axis=0, tiled=True)]
    select_n x0 -> x3, other arithmetic: none -> 12.5 us  [gather_by_bits(): grown = jnp.where(here & reach == 0, mine_first, theirs_first)]
    ppermute x0 -> x4, starting transfers between devices: none -> 7.7 us  [gather_by_bits(): theirs = lax.ppermute(grown, axis, [(d, d ^ reach) for d in range(ways)])]
    psum x1, blocking collectives: 59.2 us -> 64.6 us  [decoder_back(): summed = lax.psum(jnp.stack(tap_terms, axis=0), 'seq')]
  transfers between devices with their start and end apart: 5 -> 8, of which waited for: 1 -> 3; matrix products, arithmetic and copies ran while one was open for 8% -> 3% of each run, Pallas kernels for 0% -> 0%
where the time goes in v1:
time: 505 us; the launch traced here: 503 us
  blocking collectives  258 us (51%)
  matrix products  74.3 us (15%)
  waiting for transfers between devices  73.5 us (15%)
  other arithmetic  33.6 us (7%)
  local copies, waits for them, and re-layouts  32.8 us (6%)
  starting transfers between devices  15.8 us (3%)
  between operations  14.2 us (3%)
    all_gather x1, blocking collectives, decoder_back(): every_row = lax.all_gather(track_weight, 'seq', axis=0, tiled=True)  194 us
    ppermute x4, waiting for transfers between devices, gather_by_bits(): theirs = lax.ppermute(grown, axis, [(d, d ^ reach) for d in range(ways)])  73.5 us
    psum x1, blocking collectives, decoder_back(): summed = lax.psum(jnp.stack(tap_terms, axis=0), 'seq')  64.6 us
    dot_general x16, matrix products, block_update(): jnp.dot(expw.astype(jnp.bfloat16), key_block[:, QK:], preferred_element_t...  39.7 us
    reduce_sum x16, other arithmetic, block_update(): running_sum = running_sum * shrink + jnp.sum(expw, axis=1)  18.2 us
    dot_general x16, matrix products, block_update(): lax.dot_general(query_rows, key_block[:, :QK], (((1,), (1,)), ((), ())),...  16.7 us
    squeeze x16, local copies, waits for them, and re-layouts, attention(): lax.scan(step_fn, carry, piece.reshape(count // 128, 128, piece.shape[1]))  14.4 us
    select_n x3, other arithmetic, gather_by_bits(): grown = jnp.where(here & reach == 0, mine_first, theirs_first)  12.5 us
  transfers between devices with their start and end apart: 8, of which 3 were waited for; matrix products, arithmetic and copies ran while one was open for 3% of the time, Pallas kernels for 0%

profile of v1, /device:TPU:0, one launch (start us, length us, event | category | flops | bytes accessed | tf_op | source)
XLA Modules:
  0.0 502.7 jit_solution(72258049865572238)
XLA Ops:
  9.6 2.8 maximum_select_fusion.10
  12.4 2.9 collective-permute-start.1
  15.3 24.5 %collective-permute-done.1 = bf16[352,1536]{1,0:T(8,128)(2,1)} collective-permute-done((bf16[352,1536]{1,0:T(8,128)(2,1)}, bf16[352,1536]{1,0:T(8,128)(2,1)}, u32[]{:S(2)}, u32[]{:S(2)}) %collective-permute-start.1) | collective-permute-done | bytes 1081376 | tf_op jit(solution)/shard_map/ppermute | solution.py:17
  39.7 4.2 maximum_select_fusion.9
  45.7 47.1 %collective-permute-done.2 = bf16[704,1536]{1,0:T(8,128)(2,1)} collective-permute-done((bf16[704,1536]{1,0:T(8,128)(2,1)}, bf16[704,1536]{1,0:T(8,128)(2,1)}, u32[]{:S(2)}, u32[]{:S(2)}) %collective-permute-start.2) | collective-permute-done | bytes 2162720 | tf_op jit(solution)/shard_map/ppermute | solution.py:17
  92.8 5.5 %maximum_select_fusion.2 = bf16[1408,1536]{1,0:T(8,128)(2,1)} fusion(bf16[704,1536]{1,0:T(8,128)(2,1)} %collective-permute-done.2, bf16[704,1536]{1,0:T(8,128)(2,1)} %maximum_select_fusion.9, pred[]{:T(512)S(6)} %eq.13), kind=kLoop, calls=%fused_computation.23 | loop fusion | flops 19464192 | bytes 8650753 | tf_op jit(solution)/shard_map/jit(_where)/select_n | solution.py:20
  98.3 2.5 collective-permute-start.3
  101.5 3.9 all-to-all-start
  105.5 193.8 %all-gather = bf16[16,12,1536]{2,1,0:T(8,128)(2,1)} all-gather(bf16[1,12,1536]{2,1,0:T(8,128)(2,1)S(1)} %bitcast.29), channel_id=1, replica_groups=mesh['groups'=2,'seq'=16] {'seq'}, dimensions={0}, use_global_device_ids=true | all-gather | bytes 626688 | tf_op jit(solution)/shard_map/all_gather | solution.py:98
  301.4 3.6 gather_fusion
  307.7 2.8 collective-permute-start.4
  316.4 8.8 %multiply_reduce_fusion.3 = (f32[1536]{0:T(1024)S(1)}, f32[1536]{0:T(1024)S(1)}, f32[1536]{0:T(1024)S(1)}, f32[128]{0:T(128)S(1)}, bf16[128,1536]{1,0:T(8,128)(2,1)}, /*index=5*/f32[128,1536]{1,0:T(8,128)S(1)}) fusion(f32[144,1536]{1,0:T(8,128)S(1)} %maximum_convert_fusion, f32[1536]{0:T(1024)S(1)} %get-tuple-element.82, f32[1536]{0:T(1024)} %get-tuple-element.83, ...), kind=kOutput, calls=%fused_computation.46 | convolution fusion | flops 1153101184 | bytes 12947969 | tf_op jit(solution)/shard_map/dot_general | solution.py:133
  327.3 2.5 convolution_convert_fusion.1
  330.9 64.6 %psum.7 = f32[3,1536]{1,0:T(4,128)S(1)} all-reduce(f32[3,1536]{1,0:T(4,128)S(1)} %pad_maximum_fusion), channel_id=1, replica_groups=mesh['groups'=2,'seq'=16] {'seq'}, use_global_device_ids=true, to_apply=%region_8.9 | all-reduce | flops 4608 | bytes 36864 | tf_op jit(solution)/shard_map/psum | solution.py:113
  396.1 2.6 copy.21
  398.6 89.4 %while.15 = (s32[]{:T(128)}, f32[1024]{0:T(1024)S(1)}, f32[1024]{0:T(1024)S(1)}, f32[1024,192]{0,1:T(8,128)}, bf16[16,128,320]{2,1,0:T(8,128)(2,1)}, /*index=5*/bf16[1024,128]{1,0:T(8,128)(2,1)S(1)}, s32[]{:T(128)}, s32[]{:T(128)}) while((s32[]{:T(128)}, f32[1024]{0:T(1024)S(1)}, f32[1024]{0:T(1024)S(1)}, f32[1024,192]{0,1:T(8,128)}, ...), condition=%wide.region_4.5_spmd.clone, body=%wide.region_1.4_spmd.clone.sunk | while | flops 85267456 | bytes 3735653 | solution.py:84
  407.1 2.5 convolution_add_fusion.3
  412.7 2.5 convolution_add_fusion.3
  418.3 2.5 convolution_add_fusion.3
  423.9 2.5 convolution_add_fusion.3
  429.5 2.5 convolution_add_fusion.3
  435.1 2.5 convolution_add_fusion.3
  440.7 2.5 convolution_add_fusion.3
  446.3 2.5 convolution_add_fusion.3
  451.9 2.5 convolution_add_fusion.3
  457.5 2.5 convolution_add_fusion.3
  463.1 2.5 convolution_add_fusion.3
  468.7 2.5 convolution_add_fusion.3
  474.3 2.5 convolution_add_fusion.3
  479.9 2.5 convolution_add_fusion.3
  485.5 2.5 convolution_add_fusion.3
  491.8 4.1 fusion.17
  (152 shorter events, 74.8 us)
Async XLA Ops:
  7.2 320.1 %copy-start = (bf16[1536,1024]{1,0:T(8,128)(2,1)S(1)}, bf16[1536,1024]{1,0:T(8,128)(2,1)}, u32[]{:S(2)}) copy-start(bf16[1536,1024]{1,0:T(8,128)(2,1)} %param.16) | copy-start | bytes 9437188
  7.2 2.4 collective-permute-start
  12.4 27.4 %collective-permute-start.1 = (bf16[352,1536]{1,0:T(8,128)(2,1)}, bf16[352,1536]{1,0:T(8,128)(2,1)}, u32[]{:S(2)}, u32[]{:S(2)}) collective-permute-start(bf16[352,1536]{1,0:T(8,128)(2,1)} %maximum_select_fusion.10), channel_id=1, source_target_pairs={{0,2},{1,3},{2,0},{3,1},{4,6},{5,7},{6,4},{7,5},{8,10},{9,11},{10,... | collective-permute-start | bytes 3244040 | tf_op jit(solution)/shard_map/ppermute | solution.py:17
  43.9 48.9 %collective-permute-start.2 = (bf16[704,1536]{1,0:T(8,128)(2,1)}, bf16[704,1536]{1,0:T(8,128)(2,1)}, u32[]{:S(2)}, u32[]{:S(2)}) collective-permute-start(bf16[704,1536]{1,0:T(8,128)(2,1)} %maximum_select_fusion.9), channel_id=1, source_target_pairs={{0,4},{1,5},{2,6},{3,7},{4,0},{5,1},{6,2},{7,3},{8,12},{9,13},{10,... | collective-permute-start | bytes 6488072 | tf_op jit(solution)/shard_map/ppermute | solution.py:17
  45.7 55.1 %copy-start.3 = (bf16[2048,12]{0,1:T(8,128)(2,1)S(1)}, bf16[2048,12]{0,1:T(8,128)(2,1)}, u32[]{:S(2)}) copy-start(bf16[2048,12]{0,1:T(8,128)(2,1)} %param.21) | copy-start | bytes 147460
  45.7 59.7 %copy-start.4 = (bf16[12,1536]{1,0:T(8,128)(2,1)S(1)}, bf16[12,1536]{1,0:T(8,128)(2,1)}, u32[]{:S(2)}) copy-start(bf16[12,1536]{1,0:T(8,128)(2,1)} %param.20) | copy-start | bytes 110596
  45.7 255.6 %copy-start.7 = (s32[192]{0:T(256)S(1)}, s32[192]{0:T(256)}, u32[]{:S(2)}) copy-start(s32[192]{0:T(256)} %param.23) | copy-start | bytes 2308
  45.7 255.6 %copy-start.6 = (s32[192]{0:T(256)S(1)}, s32[192]{0:T(256)}, u32[]{:S(2)}) copy-start(s32[192]{0:T(256)} %param.22) | copy-start | bytes 2308
  98.3 218.1 %collective-permute-start.3 = (bf16[1408,1536]{1,0:T(8,128)(2,1)}, bf16[1408,1536]{1,0:T(8,128)(2,1)}, u32[]{:S(2)}, u32[]{:S(2)}) collective-permute-start(bf16[1408,1536]{1,0:T(8,128)(2,1)} %maximum_select_fusion.2), channel_id=1, source_target_pairs={{0,8},{1,9},{2,10},{3,11},{4,12},{5,13},{6,14},{7,15},{8,0},{9,1},... | collective-permute-start | bytes 12976136 | tf_op jit(solution)/shard_map/ppermute | solution.py:17
  101.5 203.5 %all-to-all-start = ((bf16[16,128,12]{1,2,0:T(8,128)(2,1)}), bf16[16,128,12]{1,2,0:T(8,128)(2,1)S(1)}, u32[]{:S(2)}, u32[]{:S(2)}) async-start(bf16[16,128,12]{1,2,0:T(8,128)(2,1)} %copy.20), calls=%async_computation | async-start | bytes 131072 | tf_op jit(solution)/shard_map/all_to_all | solution.py:96
  105.4 290.6 %all-gather.3.cloned.1.call-start = ((), (), s32[]{:S(2)}) async-start(), calls=%async_computation.1 | async-start | bytes 1392640 | tf_op jit(solution)/shard_map/all_gather | solution.py:78
  307.7 7.8 %collective-permute-start.4 = (bf16[8,1536]{1,0:T(8,128)(2,1)}, bf16[8,1536]{1,0:T(8,128)(2,1)}, u32[]{:S(2)}, u32[]{:S(2)}) collective-permute-start(bf16[8,1536]{1,0:T(8,128)(2,1)} %get-tuple-element.101), channel_id=1, source_target_pairs={{0,1},{1,2},{2,3},{3,4},{4,5},{5,6},{6,7},{7,8},{8,9},{9,10},{10,1... | collective-permute-start | bytes 73736 | tf_op jit(solution)/shard_map/ppermute | solution.py:33
  310.6 5.0 collective-permute-start.5
  316.4 9.7 %copy-start.2 = (bf16[1536,320]{0,1:T(8,128)(2,1)S(1)}, bf16[1536,320]{0,1:T(8,128)(2,1)}, u32[]{:S(2)}) copy-start(bf16[1536,320]{0,1:T(8,128)(2,1)} %param.17) | copy-start | bytes 2949124
  316.4 9.7 %copy-start.5 = (f32[1536]{0:T(1024)S(1)}, f32[1536]{0:T(1024)}, u32[]{:S(2)}) copy-start(f32[1536]{0:T(1024)} %param.15) | copy-start | bytes 18436
  325.2 0.9 copy-start.1
Sparse Core Ops, SparseCore 0:
  327.3 41.9 all-gather.2
